TPU v7x, 128 devices: a whole 4x4x4 slice. The times are simulated.
128 devices in a mesh: section: 4 (over y), dp: 2 (over core), expert: 16 (over x, z).
Axes of the slice: x: 4, y: 4, z: 4, core: 2. Of those that a mesh axis runs over, the one named last changes fastest.
Arguments:
- stashed: bfloat16 [4, 6144, 2048], P('section', ('dp', 'expert')), may hold values from -6 to 6
- expert_ids: int32 [4, 6144, 8], P('section', ('dp', 'expert')), may hold values from 0 to 63, all different within a row; in each aligned block of 192 rows (0 to 191, 192 to 383, ..., all dimensions but the last counted through in order) at most 48 rows name the same one
- route_probs: float32 [4, 6144, 8], P('section', ('dp', 'expert')), may hold values from 0.02 to 1
- w_gate: bfloat16 [4, 64, 2048, 768], P('section', ('dp', 'expert')), may hold values from -0.125 to 0.125
- w_up: bfloat16 [4, 64, 2048, 768], P('section', ('dp', 'expert')), may hold values from -0.125 to 0.125
- w_down: bfloat16 [4, 64, 768, 2048], P('section', ('dp', 'expert')), may hold values from -0.21875 to 0.21875
Outputs:
- handed: bfloat16 [4, 6144, 2048], P('section', ('dp', 'expert'))
- balance: float32 [4], P('section')
Inputs may be any that keep to these rules, and one draw needn't show every extreme that they name: `expert_ids`: each token names 8 different experts; among the tokens of one device (aligned blocks of 192 tokens) no expert is named more than 48 times, and in every draw some expert is named exactly 48 times in some block.
All inputs are finite; a program needn't handle non-finite values.
Results may differ from a plain program's by a relative error of at most 0.0032.
Values may be sent and summed in bfloat16 or wider, within the bound.
No kernel may reach another device: no remote copies, remote signals or barrier semaphores. Data moves between devices by JAX's collectives and lax.ppermute only.
A program may use at most 128 MiB of HBM per device.

v0:
```python
import jax
import jax.numpy as jnp
from jax import lax
from jax.sharding import PartitionSpec as P


def passed_along(value, axis, steps):
    count = lax.axis_size(axis)
    pairs = [(source, (source + steps) % count) for source in range(count)]
    return lax.ppermute(value, axis, pairs)


def expert_rows(received, gate_w, up_w, down_w, form_in, form_out):
    gate_act = jnp.einsum(form_in, received, gate_w, preferred_element_type=jnp.float32)
    up_act = jnp.einsum(form_in, received, up_w, preferred_element_type=jnp.float32)
    hidden = (jax.nn.silu(gate_act) * up_act).astype(jnp.bfloat16)
    return jnp.einsum(form_out, hidden, down_w, preferred_element_type=jnp.float32).astype(
        jnp.bfloat16
    )


def per_device(stashed, expert_ids, route_probs, w_gate, w_up, w_down):
    tokens_in = stashed[0]
    choice_ids = expert_ids[0]
    probs = route_probs[0]
    gate_w = w_gate[0]
    up_w = w_up[0]
    down_w = w_down[0]
    expert_count = lax.axis_size("expert")
    dp_count = lax.axis_size("dp")
    local_count = gate_w.shape[0]
    all_experts = dp_count * expert_count * local_count
    token_count, top_count = choice_ids.shape
    model_width = tokens_in.shape[1]
    capacity = 2 * token_count * top_count // all_experts
    inputs = tokens_in.astype(jnp.float32)
    normed = (inputs * lax.rsqrt(jnp.mean(inputs * inputs, axis=-1, keepdims=True) + 1e-06)).astype(
        jnp.bfloat16
    )
    flat_ids = choice_ids.reshape(-1)
    labels = jnp.arange(all_experts, dtype=jnp.int32)
    onehot = (flat_ids[:, None] == labels[None, :]).astype(jnp.int32)
    running = jnp.cumsum(onehot, axis=0)
    position = jnp.sum(running * onehot, axis=1) - 1
    slot_rows = flat_ids * capacity + position
    sent_rows = (
        jnp.zeros((all_experts * capacity, model_width), jnp.bfloat16)
        .at[slot_rows]
        .set(jnp.repeat(normed, top_count, axis=0))
    )
    arranged = sent_rows.reshape(dp_count * expert_count, local_count, capacity, model_width)
    received = lax.all_to_all(arranged, ("dp", "expert"), split_axis=0, concat_axis=0, tiled=True)
    result = expert_rows(received, gate_w, up_w, down_w, "secd,edf->secf", "secf,efd->secd")
    returned = lax.all_to_all(result, ("dp", "expert"), split_axis=0, concat_axis=0, tiled=True)
    picked = returned.reshape(all_experts * capacity, model_width)[slot_rows]
    picked = picked.reshape(token_count, top_count, model_width).astype(jnp.float32)
    weights = probs / jnp.sum(probs, axis=-1, keepdims=True)
    mixture = jnp.sum(weights[:, :, None] * picked, axis=1)
    layer_out = (inputs + mixture).astype(jnp.bfloat16)
    counts = jnp.sum(onehot, axis=0).astype(jnp.float32)
    mass = jnp.dot(weights.reshape(-1), onehot.astype(jnp.float32), precision=lax.Precision.HIGHEST)
    counts_all, mass_all = lax.psum((counts, mass), ("dp", "expert"))
    tokens_all = token_count * dp_count * expert_count
    loss = all_experts * jnp.sum(counts_all / (tokens_all * top_count) * (mass_all / tokens_all))
    handed = passed_along(layer_out, "section", 1)
    return (handed[None], loss.reshape(1))


def solution(mesh):
    placed = (
        P("section", ("dp", "expert"), None),
        P("section", ("dp", "expert"), None),
        P("section", ("dp", "expert"), None),
        P("section", ("dp", "expert"), None, None),
        P("section", ("dp", "expert"), None, None),
        P("section", ("dp", "expert"), None, None),
    )
    return jax.shard_map(
        per_device,
        mesh=mesh,
        in_specs=placed,
        out_specs=(P("section", ("dp", "expert"), None), P("section")),
        check_vma=False,
    )
```

profile of v0, /device:TPU:2, one launch (start us, length us, event | category | flops | bytes accessed | tf_op | source)
XLA Modules:
  0.0 558.4 jit_solution(3848793365307210415)
XLA Ops:
  0.6 0.8 copy.21
  1.7 0.7 broadcast_multiply_fusion
  2.4 18.1 %reduce-window.6 = s32[64,12,128]{2,1,0:T(8,128)S(1)} reduce-window(s32[64,12,128]{2,1,0:T(8,128)S(1)} %fusion.29, s32[]{:T(128)} %constant.9.clone.1), window={size=1x1x128 pad=0_0x0_0x127_0}, to_apply=%region_1.0 | reduce-window | flops 12484608 | bytes 786436 | tf_op jit(solution)/shard_map/reduce-window
  20.5 0.2 slice.10
  20.7 0.3 copy.23
  21.3 0.2 convert_reduce_fusion
  21.8 1.4 fusion.26
  23.2 1.3 fusion.27
  24.5 16.3 %scatter_custom_fusion = bf16[3072,2048]{1,0:T(8,128)(2,1)} fusion(s32[1536]{0:T(1024)S(1)} %fusion.33, bf16[]{:T(256)} %constant.8.clone.1, bf16[192,2048]{1,0:T(8,128)(2,1)S(1)} %fusion.27), kind=kCustom, calls=%fused_computation.19 | custom fusion | bytes 13369346 | tf_op jit(solution)/shard_map/scatter | solution.py:49
  40.9 149.1 %all_to_all.10 = bf16[32,2,48,2048]{3,2,1,0:T(8,128)(2,1)S(1)} all-to-all(bf16[32,2,48,2048]{3,2,1,0:T(8,128)(2,1)} %bitcast.78), channel_id=1, replica_groups=mesh['section'=4,'dp'=2,'expert'=16] {'dp','expert'}, dimensions={0} | all-to-all | bytes 25165824 | tf_op jit(solution)/shard_map/all_to_all | solution.py:52
  189.9 4.5 copy-done
  194.4 14.1 %fusion.1 = f32[2,32,48,768]{3,2,1,0:T(8,128)} fusion(bf16[32,2,48,2048]{3,2,1,0:T(8,128)(2,1)S(1)} %all_to_all.10, bf16[1,2,2048,768]{3,2,1,0:T(8,128)(2,1)} %param.10), kind=kOutput, calls=%fused_computation.5 | convolution fusion | flops 9663676416 | bytes 28311552 | tf_op jit(solution)/shard_map/secd,edf->secf/dot_general | solution.py:15
  208.4 29.3 %convert_bitcast_fusion = bf16[32,2,48,2048]{3,2,0,1:T(8,128)(2,1)} fusion(bf16[1,2,768,2048]{3,2,1,0:T(8,128)(2,1)} %param.11, f32[2,32,48,768]{3,2,1,0:T(8,128)} %fusion.1, bf16[32,2,48,2048]{3,2,1,0:T(8,128)(2,1)} %copy-done, bf16[1,2,2048,768]{3,2,1,0:T(8,128)(2,1)} %param.9), kind=kOutput, calls=%fused_computation.4 | convolution fusion | flops 19347800064 | bytes 47185920 | tf_op jit(solution)/shard_map/secf,efd->secd/dot_general | solution.py:17
  237.8 10.8 %copy.27 = bf16[32,2,48,2048]{3,2,1,0:T(8,128)(2,1)} copy(bf16[32,2,48,2048]{3,2,0,1:T(8,128)(2,1)} %convert_bitcast_fusion) | data formatting | bytes 25165824 | tf_op jit(solution)/shard_map/convert_element_type | solution.py:17
  248.6 5.4 all-to-all-start.1
  254.2 194.4 %all-to-all-done.1 = bf16[32,2,48,2048]{3,2,1,0:T(8,128)(2,1)} async-done(((bf16[32,2,48,2048]{3,2,1,0:T(8,128)(2,1)}), bf16[32,2,48,2048]{3,2,1,0:T(8,128)(2,1)}, u32[]{:S(2)}, u32[]{:S(2)}) %all-to-all-start.1) | async-done | bytes 12582944 | tf_op jit(solution)/shard_map/all_to_all | solution.py:54
  448.6 19.0 %gather_fusion = bf16[1536,2048]{1,0:T(8,128)(2,1)} fusion(bf16[3072,2048]{1,0:T(8,128)(2,1)} %bitcast.19, s32[2048]{0:T(1024)S(1)} %pad_clamp_fusion), kind=kCustom, calls=%fused_computation | custom fusion | bytes 12589056 | tf_op jit(solution)/shard_map/gather | solution.py:55
  467.6 9.2 %fusion = f32[192,2048]{1,0:T(8,128)S(1)} fusion(bf16[1536,2048]{1,0:T(8,128)(2,1)} %gather_fusion, f32[192,8]{1,0:T(8,128)S(1)} %copy.19), kind=kLoop, calls=%fused_computation.3 | loop fusion | flops 9043968 | bytes 7870464 | tf_op jit(solution)/shard_map/reduce_sum | solution.py:58
  476.9 0.2 fusion.28
  477.1 1.7 collective-permute-start
  479.2 0.4 convolution_bitcast_fusion
  479.6 75.5 %all-reduce = (f32[64]{0:T(128)S(1)}, f32[64]{0:T(128)S(1)}) all-reduce(f32[64]{0:T(128)S(1)} %convolution_bitcast_fusion, f32[64]{0:T(128)S(1)} %convert_element_type.51), channel_id=1, replica_groups=mesh['section'=4,'dp'=2,'expert'=16] {'dp','expert'}, use_global_device_ids=true, to_apply=%region_9.10 | all-reduce | flops 128 | bytes 1024 | tf_op jit(solution)/shard_map/psum | solution.py:62
  555.1 0.6 multiply_reduce_fusion
  556.4 0.9 copy.44
  (28 shorter events, 1.4 us)
Async XLA Ops:
  189.9 4.5 copy-start
  248.6 5.5 copy-start.2
  248.6 200.0 %all-to-all-start.1 = ((bf16[32,2,48,2048]{3,2,1,0:T(8,128)(2,1)}), bf16[32,2,48,2048]{3,2,1,0:T(8,128)(2,1)}, u32[]{:S(2)}, u32[]{:S(2)}) async-start(bf16[32,2,48,2048]{3,2,1,0:T(8,128)(2,1)} %copy.27), calls=%async_computation.1 | async-start | bytes 25165824 | tf_op jit(solution)/shard_map/all_to_all | solution.py:54
  448.6 28.2 %copy-start.1 = (bf16[1,192,2048]{2,1,0:T(8,128)(2,1)S(1)}, bf16[1,192,2048]{2,1,0:T(8,128)(2,1)}, u32[]{:S(2)}) copy-start(bf16[1,192,2048]{2,1,0:T(8,128)(2,1)} %param.6) | copy-start | bytes 2359300
  477.1 79.3 %collective-permute-start = (bf16[192,2048]{1,0:T(8,128)(2,1)S(1)}, bf16[192,2048]{1,0:T(8,128)(2,1)S(1)}, u32[]{:S(2)}, u32[]{:S(2)}) collective-permute-start(bf16[192,2048]{1,0:T(8,128)(2,1)S(1)} %fusion.28), channel_id=1, source_target_pairs={{0,32},{32,64},{64,96},{96,0},{1,33},{33,65},{65,97},{97,1},{2,34}... | collective-permute-start | bytes 2359304 | tf_op jit(solution)/shard_map/ppermute | solution.py:10
where the time goes:
time: 559 us; the launch traced here: 558 us
  blocking collectives  225 us (40%)
  waiting for transfers between devices  194 us (35%)
  local copies, waits for them, and re-layouts  53.8 us (10%)
  matrix products  43.8 us (8%)
  other arithmetic  32.1 us (6%)
  starting transfers between devices  7.09 us (1%)
    all_to_all x1, waiting for transfers between devices, per_device(): lax.all_to_all(result, ('dp', 'expert'), split_axis=0, concat_axis=0, til...  194 us
    all_to_all x1, blocking collectives, per_device(): lax.all_to_all(arranged, ('dp', 'expert'), split_axis=0, concat_axis=0, t...  149 us
    psum x1, blocking collectives, per_device(): counts_all, mass_all = lax.psum((counts, mass), ('dp', 'expert'))  75.5 us
    dot_general x1, matrix products, expert_rows(): jnp.einsum(form_out, hidden, down_w, preferred_element_type=jnp.float32)  29.3 us
    gather x1, local copies, waits for them, and re-layouts, per_device(): picked = returned.reshape(all_experts * capacity, model_width)[slot_rows]  19 us
    another operation x3, other arithmetic  18.4 us
    scatter x1, local copies, waits for them, and re-layouts, per_device(): sent_rows = jnp.zeros((all_experts * capacity, model_width), jnp.bfloat16...  16.3 us
    dot_general x1, matrix products, expert_rows(): jnp.einsum(form_in, received, up_w, preferred_element_type=jnp.float32)  14.1 us
  transfers between devices with their start and end apart: 2, of which 1 were waited for; matrix products, arithmetic and copies ran while one was open for 0% of the time, Pallas kernels for 0%

commit v1 on v0

--- a/solution.py
+++ b/solution.py
@@ -59,7 +59,7 @@
     layer_out = (inputs + mixture).astype(jnp.bfloat16)
     counts = jnp.sum(onehot, axis=0).astype(jnp.float32)
     mass = jnp.dot(weights.reshape(-1), onehot.astype(jnp.float32), precision=lax.Precision.HIGHEST)
-    counts_all, mass_all = lax.psum((counts, mass), ("dp", "expert"))
+    counts_all, mass_all = lax.psum(lax.psum((counts, mass), "expert"), "dp")
     tokens_all = token_count * dp_count * expert_count
     loss = all_experts * jnp.sum(counts_all / (tokens_all * top_count) * (mass_all / tokens_all))
     handed = passed_along(layer_out, "section", 1)

time: 559 us -> 534 us (0.955)
  blocking collectives: 225 us -> 198 us
    psum x1 -> x2, blocking collectives: 75.5 us -> 48.6 us  [per_device(): counts_all, mass_all = lax.psum(lax.psum((counts, mass), 'expert'), 'dp')]
where the time goes in v1:
time: 534 us; the launch traced here: 532 us
  blocking collectives  198 us (37%)
  waiting for transfers between devices  194 us (36%)
  local copies, waits for them, and re-layouts  53.8 us (10%)
  matrix products  43.8 us (8%)
  other arithmetic  32.1 us (6%)
  starting transfers between devices  7.09 us (1%)
    all_to_all x1, waiting for transfers between devices, per_device(): lax.all_to_all(result, ('dp', 'expert'), split_axis=0, concat_axis=0, til...  194 us
    all_to_all x1, blocking collectives, per_device(): lax.all_to_all(arranged, ('dp', 'expert'), split_axis=0, concat_axis=0, t...  149 us
    psum x2, blocking collectives, per_device(): counts_all, mass_all = lax.psum(lax.psum((counts, mass), 'expert'), 'dp')  48.6 us
    dot_general x1, matrix products, expert_rows(): jnp.einsum(form_out, hidden, down_w, preferred_element_type=jnp.float32)  29.3 us
    gather x1, local copies, waits for them, and re-layouts, per_device(): picked = returned.reshape(all_experts * capacity, model_width)[slot_rows]  19 us
    another operation x3, other arithmetic  18.4 us
    scatter x1, local copies, waits for them, and re-layouts, per_device(): sent_rows = jnp.zeros((all_experts * capacity, model_width), jnp.bfloat16...  16.3 us
    dot_general x1, matrix products, expert_rows(): jnp.einsum(form_in, received, up_w, preferred_element_type=jnp.float32)  14.1 us
  transfers between devices with their start and end apart: 2, of which 1 were waited for; matrix products, arithmetic and copies ran while one was open for 0% of the time, Pallas kernels for 0%

profile of v1, /device:TPU:2, one launch (start us, length us, event | category | flops | bytes accessed | tf_op | source)
XLA Modules:
  0.0 531.5 jit_solution(4934498667778157854)
XLA Ops:
  0.6 0.8 copy.21
  1.7 0.7 broadcast_multiply_fusion
  2.4 18.1 %reduce-window.6 = s32[64,12,128]{2,1,0:T(8,128)S(1)} reduce-window(s32[64,12,128]{2,1,0:T(8,128)S(1)} %fusion.29, s32[]{:T(128)} %constant.9.clone.1), window={size=1x1x128 pad=0_0x0_0x127_0}, to_apply=%region_1.0 | reduce-window | flops 12484608 | bytes 786436 | tf_op jit(solution)/shard_map/reduce-window
  20.5 0.2 slice.10
  20.7 0.3 copy.23
  21.3 0.2 convert_reduce_fusion
  21.8 1.4 fusion.26
  23.2 1.3 fusion.27
  24.5 16.3 %scatter_custom_fusion = bf16[3072,2048]{1,0:T(8,128)(2,1)} fusion(s32[1536]{0:T(1024)S(1)} %fusion.33, bf16[]{:T(256)} %constant.8.clone.1, bf16[192,2048]{1,0:T(8,128)(2,1)S(1)} %fusion.27), kind=kCustom, calls=%fused_computation.19 | custom fusion | bytes 13369346 | tf_op jit(solution)/shard_map/scatter | solution.py:49
  40.9 149.1 %all_to_all.10 = bf16[32,2,48,2048]{3,2,1,0:T(8,128)(2,1)S(1)} all-to-all(bf16[32,2,48,2048]{3,2,1,0:T(8,128)(2,1)} %bitcast.78), channel_id=1, replica_groups=mesh['section'=4,'dp'=2,'expert'=16] {'dp','expert'}, dimensions={0} | all-to-all | bytes 25165824 | tf_op jit(solution)/shard_map/all_to_all | solution.py:52
  189.9 4.5 copy-done
  194.4 14.1 %fusion.1 = f32[2,32,48,768]{3,2,1,0:T(8,128)} fusion(bf16[32,2,48,2048]{3,2,1,0:T(8,128)(2,1)S(1)} %all_to_all.10, bf16[1,2,2048,768]{3,2,1,0:T(8,128)(2,1)} %param.10), kind=kOutput, calls=%fused_computation.5 | convolution fusion | flops 9663676416 | bytes 28311552 | tf_op jit(solution)/shard_map/secd,edf->secf/dot_general | solution.py:15
  208.4 29.3 %convert_bitcast_fusion = bf16[32,2,48,2048]{3,2,0,1:T(8,128)(2,1)} fusion(bf16[1,2,768,2048]{3,2,1,0:T(8,128)(2,1)} %param.11, f32[2,32,48,768]{3,2,1,0:T(8,128)} %fusion.1, bf16[32,2,48,2048]{3,2,1,0:T(8,128)(2,1)} %copy-done, bf16[1,2,2048,768]{3,2,1,0:T(8,128)(2,1)} %param.9), kind=kOutput, calls=%fused_computation.4 | convolution fusion | flops 19347800064 | bytes 47185920 | tf_op jit(solution)/shard_map/secf,efd->secd/dot_general | solution.py:17
  237.8 10.8 %copy.27 = bf16[32,2,48,2048]{3,2,1,0:T(8,128)(2,1)} copy(bf16[32,2,48,2048]{3,2,0,1:T(8,128)(2,1)} %convert_bitcast_fusion) | data formatting | bytes 25165824 | tf_op jit(solution)/shard_map/convert_element_type | solution.py:17
  248.6 5.4 %all-to-all-start.1 = ((bf16[32,2,48,2048]{3,2,1,0:T(8,128)(2,1)}), bf16[32,2,48,2048]{3,2,1,0:T(8,128)(2,1)}, u32[]{:S(2)}, u32[]{:S(2)}) async-start(bf16[32,2,48,2048]{3,2,1,0:T(8,128)(2,1)} %copy.27), calls=%async_computation.1 | async-start | bytes 25165824 | tf_op jit(solution)/shard_map/all_to_all | solution.py:54
  254.2 194.4 %all-to-all-done.1 = bf16[32,2,48,2048]{3,2,1,0:T(8,128)(2,1)} async-done(((bf16[32,2,48,2048]{3,2,1,0:T(8,128)(2,1)}), bf16[32,2,48,2048]{3,2,1,0:T(8,128)(2,1)}, u32[]{:S(2)}, u32[]{:S(2)}) %all-to-all-start.1) | async-done | bytes 12582944 | tf_op jit(solution)/shard_map/all_to_all | solution.py:54
  448.6 19.0 %gather_fusion = bf16[1536,2048]{1,0:T(8,128)(2,1)} fusion(bf16[3072,2048]{1,0:T(8,128)(2,1)} %bitcast.19, s32[2048]{0:T(1024)S(1)} %pad_clamp_fusion), kind=kCustom, calls=%fused_computation | custom fusion | bytes 12589056 | tf_op jit(solution)/shard_map/gather | solution.py:55
  467.6 9.2 %fusion = f32[192,2048]{1,0:T(8,128)S(1)} fusion(bf16[1536,2048]{1,0:T(8,128)(2,1)} %gather_fusion, f32[192,8]{1,0:T(8,128)S(1)} %copy.19), kind=kLoop, calls=%fused_computation.3 | loop fusion | flops 9043968 | bytes 7870464 | tf_op jit(solution)/shard_map/reduce_sum | solution.py:58
  477.1 1.7 collective-permute-start
  479.2 0.4 convolution_bitcast_fusion
  479.6 46.2 %all-reduce = (f32[64]{0:T(128)S(1)}, f32[64]{0:T(128)S(1)}) all-reduce(f32[64]{0:T(128)S(1)} %convolution_bitcast_fusion, f32[64]{0:T(128)S(1)} %convert_element_type.51), channel_id=1, replica_groups=mesh['section'=4,'dp'=2,'expert'=16] {'expert'}, use_global_device_ids=true, to_apply=%region_10.11 | all-reduce | flops 128 | bytes 1024 | tf_op jit(solution)/shard_map/psum | solution.py:62
  525.8 2.5 all-reduce.1
  528.2 0.6 multiply_reduce_fusion
  529.5 0.9 copy.44
  (29 shorter events, 1.6 us)
Async XLA Ops:
  189.9 4.5 copy-start
  248.6 5.5 %copy-start.2 = (f32[1,192,8]{1,2,0:T(8,128)S(1)}, f32[1,192,8]{1,2,0:T(8,128)}, u32[]{:S(2)}) copy-start(f32[1,192,8]{1,2,0:T(8,128)} %param.8) | copy-start | bytes 18436
  248.6 200.0 %all-to-all-start.1 = ((bf16[32,2,48,2048]{3,2,1,0:T(8,128)(2,1)}), bf16[32,2,48,2048]{3,2,1,0:T(8,128)(2,1)}, u32[]{:S(2)}, u32[]{:S(2)}) async-start(bf16[32,2,48,2048]{3,2,1,0:T(8,128)(2,1)} %copy.27), calls=%async_computation.1 | async-start | bytes 25165824 | tf_op jit(solution)/shard_map/all_to_all | solution.py:54
  448.6 28.2 %copy-start.1 = (bf16[1,192,2048]{2,1,0:T(8,128)(2,1)S(1)}, bf16[1,192,2048]{2,1,0:T(8,128)(2,1)}, u32[]{:S(2)}) copy-start(bf16[1,192,2048]{2,1,0:T(8,128)(2,1)} %param.6) | copy-start | bytes 2359300
  477.1 52.4 %collective-permute-start = (bf16[192,2048]{1,0:T(8,128)(2,1)S(1)}, bf16[192,2048]{1,0:T(8,128)(2,1)S(1)}, u32[]{:S(2)}, u32[]{:S(2)}) collective-permute-start(bf16[192,2048]{1,0:T(8,128)(2,1)S(1)} %fusion.28), channel_id=1, source_target_pairs={{0,32},{32,64},{64,96},{96,0},{1,33},{33,65},{65,97},{97,1},{2,34}... | collective-permute-start | bytes 2359304 | tf_op jit(solution)/shard_map/ppermute | solution.py:10
